TPU v7x, 256 devices: a whole 4x4x8 slice. The times are simulated.
256 devices in a mesh: pipe: 4 (over x), seq: 16 (over z, core), chan: 4 (over y).
Axes of the slice: x: 4, y: 4, z: 8, core: 2. Of those that a mesh axis runs over, the one named last changes fastest.
Arguments:
- signal: bfloat16 [4, 4096, 2048], P('pipe', 'seq', 'chan'), may hold values from -6 to 6
- gate_value: bfloat16 [4, 4096, 2048], P('pipe', 'seq', 'chan'), may hold values from -6 to 6
- grad_out: bfloat16 [4, 4096, 2048], P('pipe', 'seq', 'chan'), may hold values from -1.5 to 1.5
- long_filter: bfloat16 [4, 4096, 2048], P('pipe', 'seq', 'chan'), may hold values from -0.09375 to 0.09375
- weight: bfloat16 [4, 4096, 2048], P('pipe', None, 'chan'), may hold values from -0.125 to 0.125
Outputs:
- gate_grad: bfloat16 [4, 4096, 2048], P('pipe', 'seq', 'chan')
- filter_grad: float32 [4, 4096, 2048], P('pipe', 'seq', 'chan')
- input_grad: bfloat16 [4, 4096, 4096], P('pipe', 'seq', 'chan')
All inputs are finite; a program needn't handle non-finite values.
Results may differ from a plain program's by a relative error of at most 0.02.
Values may be sent and summed in bfloat16 or wider, within the bound.
No kernel may reach another device: no remote copies, remote signals or barrier semaphores. Data moves between devices by JAX's collectives and lax.ppermute only.
A program may use at most 128 MiB of HBM per device.

v0:
```python
import math
import jax
import jax.numpy as jnp
from jax import lax
from jax.sharding import PartitionSpec as P

HIGHEST = lax.Precision.HIGHEST
HIGHER = lax.Precision.HIGH


def passed_along(x, axis, by):
    length = lax.axis_size(axis)
    return lax.ppermute(x, axis, [(i, (i + by) % length) for i in range(length)])


def make_tables(panel_len):
    span_len = 2 * panel_len
    row_index = lax.broadcasted_iota(jnp.int32, (span_len, panel_len), 0)
    col_index = lax.broadcasted_iota(jnp.int32, (span_len, panel_len), 1)
    frequency = jnp.where(row_index <= panel_len, row_index, row_index - panel_len)
    angles = (frequency * col_index % span_len).astype(jnp.float32) * (2.0 * math.pi / span_len)
    forward_table = jnp.where(row_index <= panel_len, jnp.cos(angles), -jnp.sin(angles))
    end_rows = jnp.logical_or(row_index == 0, row_index == panel_len)
    weights = jnp.where(end_rows, 1.0, 2.0) / span_len
    inverse_table = (forward_table * weights).T
    return (forward_table, inverse_table)


def make_parity(panel_len):
    row_index = lax.broadcasted_iota(jnp.int32, (2 * panel_len, 1), 0)
    frequency = jnp.where(row_index <= panel_len, row_index, row_index - panel_len)
    return (1 - 2 * (frequency % 2)).astype(jnp.float32)


def spec_product(left_spec, right_spec, interior, conjugate):
    panel_len = left_spec.shape[0] // 2
    left_real, left_imag = (left_spec[:panel_len], left_spec[panel_len:])
    right_real, right_imag = (right_spec[:panel_len], right_spec[panel_len:])
    if conjugate:
        right_imag = right_imag * (1.0 - 2.0 * interior)
    real_part = left_real * right_real - interior * left_imag * right_imag
    imag_part = (
        interior * (left_real * right_imag + left_imag * right_real)
        + (1.0 - interior) * left_imag * right_imag
    )
    return jnp.concatenate([real_part, imag_part], axis=0)


def on_device(signal, gate_value, grad_out, long_filter, weight):
    panel_len = signal.shape[1]
    chan_width = signal.shape[2]
    span_len = 2 * panel_len
    panel_count = lax.axis_size("seq")
    my_panel = lax.axis_index("seq")
    forward_table, inverse_table = make_tables(panel_len)
    parity = make_parity(panel_len)
    interior = (lax.broadcasted_iota(jnp.int32, (panel_len, 1), 0) != 0).astype(jnp.float32)
    gated = (gate_value[0].astype(jnp.float32) * grad_out[0].astype(jnp.float32)).astype(
        jnp.bfloat16
    )
    signals, gateds, filters = (
        lax.all_gather(signal, "seq", axis=1, tiled=True),
        lax.all_gather(gated[None], "seq", axis=1, tiled=True),
        lax.all_gather(long_filter, "seq", axis=1, tiled=True),
    )
    zero_spec = jnp.zeros((span_len, chan_width), jnp.float32)

    def spectrum(gathered, panel_at):
        panel_rows = lax.dynamic_slice_in_dim(gathered[0], panel_at * panel_len, panel_len, 0)
        return jnp.dot(forward_table, panel_rows.astype(jnp.float32), precision=HIGHER)

    def spectrum_if(use_panel, gathered, panel_at):
        return lax.cond(
            use_panel,
            lambda where_at: spectrum(gathered, where_at),
            lambda where_at: zero_spec,
            panel_at,
        )

    def invert(spectrum_in):
        return jnp.dot(inverse_table, spectrum_in, precision=HIGHEST)

    def settle(lag_parts, spectrum_in, use_panel, target):

        def add_rows(parts_now):
            row_at = jnp.maximum(target, 0)
            current = lax.dynamic_index_in_dim(parts_now, row_at, 0, keepdims=True)
            return lax.dynamic_update_index_in_dim(
                parts_now, current + invert(spectrum_in)[None], row_at, 0
            )

        return lax.cond(use_panel, add_rows, lambda parts_now: parts_now, lag_parts)

    own_gated = jnp.dot(forward_table, gated.astype(jnp.float32), precision=HIGHER)
    last_lag = jnp.maximum(my_panel, panel_count - 1 - my_panel)
    extras = (
        zero_spec,
        jnp.array(False),
        jnp.zeros((panel_count, panel_len, chan_width), jnp.float32),
    )

    def lag_step(lag_index, loop_state):
        prior_filter, forward_sum, backward_sum, extras_now = loop_state
        filter_now = spectrum(filters, lag_index)
        filter_full = filter_now + parity * prior_filter
        use_forward = lag_index <= my_panel
        use_backward = lag_index <= panel_count - 1 - my_panel
        signal_spec = spectrum_if(use_forward, signals, jnp.maximum(my_panel - lag_index, 0))
        gated_spec = spectrum_if(
            use_backward, gateds, jnp.minimum(my_panel + lag_index, panel_count - 1)
        )
        forward_sum = forward_sum + spec_product(filter_full, signal_spec, interior, False)
        backward_sum = backward_sum + spec_product(gated_spec, filter_full, interior, True)
        prior_pair, prior_flag, lag_parts = extras_now
        pair_spec = spec_product(own_gated, signal_spec, interior, True)
        ready = jnp.logical_and(lag_index >= 1, jnp.logical_or(prior_flag, use_forward))
        lag_parts = settle(lag_parts, prior_pair + parity * pair_spec, ready, lag_index - 1)
        extras_now = (pair_spec, use_forward, lag_parts)
        return (filter_now, forward_sum, backward_sum, extras_now)

    unused_filter, forward_sum, backward_sum, extras = lax.fori_loop(
        0, last_lag + 1, lag_step, (zero_spec, zero_spec, zero_spec, extras)
    )
    prior_pair, prior_flag, lag_parts = extras
    lag_parts = settle(lag_parts, prior_pair, prior_flag, last_lag)
    filter_grad = lax.psum_scatter(
        lag_parts.reshape(1, panel_count * panel_len, chan_width).astype(jnp.bfloat16),
        "seq",
        scatter_dimension=1,
        tiled=True,
    ).astype(jnp.float32)
    conv = invert(forward_sum)
    gate_grad = (grad_out[0].astype(jnp.float32) * conv).astype(jnp.bfloat16)[None]
    signal_grad = invert(backward_sum).astype(jnp.bfloat16)
    received = passed_along(signal_grad[None], "pipe", -1)
    partial_sums = lax.dot_general(
        received[0], weight[0], (((1,), (1,)), ((), ())), preferred_element_type=jnp.float32
    )
    input_grad = lax.psum_scatter(
        partial_sums[None], "chan", scatter_dimension=2, tiled=True
    ).astype(jnp.bfloat16)
    return (gate_grad, filter_grad, input_grad)


def solution(mesh):
    return jax.shard_map(
        on_device,
        mesh=mesh,
        in_specs=(
            P("pipe", "seq", "chan"),
            P("pipe", "seq", "chan"),
            P("pipe", "seq", "chan"),
            P("pipe", "seq", "chan"),
            P("pipe", None, "chan"),
        ),
        out_specs=(P("pipe", "seq", "chan"), P("pipe", "seq", "chan"), P("pipe", "seq", "chan")),
        check_vma=False,
    )
```

profile of v0, /device:TPU:1, one launch (start us, length us, event | category | flops | bytes accessed | tf_op | source)
XLA Modules:
  0.0 692.9 jit_solution(5440354241216987989)
XLA Ops:
  11.7 4.8 fusion.62
  16.4 40.3 %all-gather.8.cloned.1.call-done = bf16[1,4096,512]{2,1,0:T(8,128)(2,1)} async-done(((bf16[1,256,512]{2,1,0:T(8,128)(2,1)}), bf16[1,4096,512]{2,1,0:T(8,128)(2,1)}) %all-gather.8.cloned.1.call-update) | async-done | bytes 4194320 | tf_op jit(solution)/shard_map/all_gather | solution.py:63
  56.8 42.5 %all-gather.4.cloned.1.call-done = bf16[1,4096,512]{2,1,0:T(8,128)(2,1)} async-done(((bf16[1,256,512]{2,1,0:T(8,128)(2,1)}), bf16[1,4096,512]{2,1,0:T(8,128)(2,1)}) %all-gather.4.cloned.1.call-update) | async-done | bytes 4194320 | tf_op jit(solution)/shard_map/all_gather | solution.py:64
  99.3 42.5 %all-gather.6.cloned.1.call-done = bf16[1,4096,512]{2,1,0:T(8,128)(2,1)} async-done(((bf16[1,256,512]{2,1,0:T(8,128)(2,1)}), bf16[1,4096,512]{2,1,0:T(8,128)(2,1)}) %all-gather.6.cloned.1.call-update) | async-done | bytes 4194320 | tf_op jit(solution)/shard_map/all_gather | solution.py:62
  141.8 4.1 broadcast_in_dim.38
  149.6 290.2 %while.31 = (s32[]{:T(128)}, f32[512,512]{1,0:T(8,128)S(1)}, f32[512,512]{1,0:T(8,128)}, f32[512,512]{1,0:T(8,128)}, f32[512,512]{1,0:T(8,128)}, /*index=5*/pred...) while((s32[]{:T(128)}, f32[512,512]{1,0:T(8,128)S(1)}, ...), condition=%wide.region_7.8_spmd.clone.clone.clone, body=%wide.region_0.7_spmd.clone.clone.clone.sunk | while | flops 2027169536 | bytes 49307344 | solution.py:121
  149.6 4.7 multiply_add_fusion.5
  165.9 3.6 maximum_add_fusion.3
  169.6 4.7 multiply_add_fusion.5
  184.9 7.4 %conditional.19 = (f32[16,256,512]{1,2,0:T(8,128)}) conditional(s32[]{:T(128)} %convert_element_type.270, f32[16,256,512]{1,2,0:T(8,128)} %get-tuple-element.824, (s32[]{:T(128)}, f32[16,256,512]{1,2,0:T(8,128)}, f32[512,1]{0,1:T(1,128)S(1)}, f32[512,512]{1,0:T(8,128)S(1)}, f32[512,512]{1,0:T(8,128)}, /*index=5*/pred[256,512]{1,0:T(32,128)(4,1)S(1)}, ...), branch_computations={%region_5.5_spmd, %region_6.6_spmd} | conditional | flops 806354944 | bytes 4329508 | solution.py:92
  184.9 7.4 %fusion.15 = f32[16,256,512]{1,2,0:T(8,128)} fusion(f32[16,256,512]{1,2,0:T(8,128)} %get-tuple-element.344, s32[]{:T(128)S(6)} %max.13, f32[512,512]{1,0:T(8,128)} %get-tuple-element.346, f32[512,512]{1,0:T(8,128)S(1)} %get-tuple-element.348, pred[256,512]{1,0:T(32,128)(4,1)S(1)} %get-tuple-element.581, f32[256,512]{1,0:T(8,128)S(1)} %get-tuple-element.587, ...), kind=kOutput, calls=%fused_computation.14 | convolution fusion | flops 806354944 | bytes 4329476 | tf_op jit(solution)/shard_map/while/body/cond/branch_1_fun/dot_general | solution.py:81
  193.3 3.6 maximum_add_fusion.3
  196.9 4.7 multiply_add_fusion.5
  210.3 7.4 %conditional.19 = (f32[16,256,512]{1,2,0:T(8,128)}) conditional(s32[]{:T(128)} %convert_element_type.270, f32[16,256,512]{1,2,0:T(8,128)} %get-tuple-element.824, (s32[]{:T(128)}, f32[16,256,512]{1,2,0:T(8,128)}, f32[512,1]{0,1:T(1,128)S(1)}, f32[512,512]{1,0:T(8,128)S(1)}, f32[512,512]{1,0:T(8,128)}, /*index=5*/pred[256,512]{1,0:T(32,128)(4,1)S(1)}, ...), branch_computations={%region_5.5_spmd, %region_6.6_spmd} | conditional | flops 806354944 | bytes 4329508 | solution.py:92
  210.4 7.4 %fusion.15 = f32[16,256,512]{1,2,0:T(8,128)} fusion(f32[16,256,512]{1,2,0:T(8,128)} %get-tuple-element.344, s32[]{:T(128)S(6)} %max.13, f32[512,512]{1,0:T(8,128)} %get-tuple-element.346, f32[512,512]{1,0:T(8,128)S(1)} %get-tuple-element.348, pred[256,512]{1,0:T(32,128)(4,1)S(1)} %get-tuple-element.581, f32[256,512]{1,0:T(8,128)S(1)} %get-tuple-element.587, ...), kind=kOutput, calls=%fused_computation.14 | convolution fusion | flops 806354944 | bytes 4329476 | tf_op jit(solution)/shard_map/while/body/cond/branch_1_fun/dot_general | solution.py:81
  218.8 3.6 maximum_add_fusion.3
  222.4 4.7 multiply_add_fusion.5
  236.9 3.6 maximum_add_fusion.3
  240.6 4.7 multiply_add_fusion.5
  255.0 3.6 maximum_add_fusion.3
  258.7 4.7 multiply_add_fusion.5
  273.1 3.6 maximum_add_fusion.3
  276.8 4.7 multiply_add_fusion.5
  291.2 3.6 maximum_add_fusion.3
  294.9 4.7 multiply_add_fusion.5
  309.3 3.6 maximum_add_fusion.3
  313.0 4.7 multiply_add_fusion.5
  327.4 3.6 maximum_add_fusion.3
  331.1 4.7 multiply_add_fusion.5
  345.6 3.6 maximum_add_fusion.3
  349.2 4.7 multiply_add_fusion.5
  363.7 3.6 maximum_add_fusion.3
  367.3 4.7 multiply_add_fusion.5
  381.8 3.6 maximum_add_fusion.3
  385.4 4.7 multiply_add_fusion.5
  399.9 3.6 maximum_add_fusion.3
  403.5 4.7 multiply_add_fusion.5
  418.0 3.6 maximum_add_fusion.3
  421.6 4.7 multiply_add_fusion.5
  436.1 3.6 maximum_add_fusion.3
  439.8 9.3 %conditional.4 = (f32[16,256,512]{2,1,0:T(8,128)}) conditional(s32[]{:T(128)} %convert_element_type.151, (f32[16,256,512]{1,2,0:T(8,128)}) %tuple.109, (s32[]{:T(128)}, f32[16,256,512]{1,2,0:T(8,128)}, pred[256,512]{1,0:T(32,128)(4,1)S(1)}, f32[512,512]{1,0:T(8,128)}, f32[512]{0:T(512)S(1)}, /*index=5*/f32[256,512]{1,0:T(8,128)}, ...), branch_computations={%region_8.9_spmd, %region_9.10_spmd} | conditional | flops 805830656 | bytes 26347600 | solution.py:92
  439.8 9.2 %copy.46 = f32[16,256,512]{2,1,0:T(8,128)} copy(f32[16,256,512]{1,2,0:T(8,128)} %get-tuple-element.589) | data formatting | bytes 16777216 | tf_op jit(solution)/shard_map/while | solution.py:121
  449.0 5.9 convert_element_type.152
  462.2 3.3 collective-permute-done
  465.5 5.5 convolution_bitcast_fusion.5
  472.3 4.0 fusion.50
  476.2 154.6 %reduce-scatter.3.cloned.1.call-done = bf16[1,256,512]{2,1,0:T(8,128)(2,1)} async-done(((bf16[1,4096,512]{2,1,0:T(8,128)(2,1)}), bf16[1,256,512]{2,1,0:T(8,128)(2,1)}) %reduce-scatter.3.cloned.1.call-update) | async-done | bytes 262160 | tf_op jit(solution)/shard_map/reduce_scatter | solution.py:126
  632.7 51.6 %reduce-scatter.5.cloned.1.call-done = f32[1,256,1024]{2,1,0:T(8,128)} async-done(((f32[1,256,4096]{2,1,0:T(8,128)}), f32[1,256,1024]{2,1,0:T(8,128)}) %reduce-scatter.5.cloned.1.call-update) | async-done | bytes 1048592 | tf_op jit(solution)/shard_map/reduce_scatter | solution.py:139
  (392 shorter events, 204.1 us)
Async XLA Ops:
  7.2 49.6 %all-gather.8.cloned.1.call-start = ((), (), s32[]{:S(2)}) async-start(), calls=%async_computation.4 | async-start | bytes 4456448 | tf_op jit(solution)/shard_map/all_gather | solution.py:63
  9.0 90.3 %all-gather.4.cloned.1.call-start = ((), (), s32[]{:S(2)}) async-start(), calls=%async_computation.2 | async-start | bytes 4456448 | tf_op jit(solution)/shard_map/all_gather | solution.py:64
  9.8 132.1 %all-gather.6.cloned.1.call-start = ((), (), s32[]{:S(2)}) async-start(), calls=%async_computation.3 | async-start | bytes 4456448 | tf_op jit(solution)/shard_map/all_gather | solution.py:62
  10.5 620.3 %reduce-scatter.3.cloned.1.call-start = ((), (), s32[]{:S(2)}) async-start(), calls=%async_computation.5 | async-start | bytes 4456448 | tf_op jit(solution)/shard_map/reduce_scatter | solution.py:126
  154.3 2.2 copy-start.5
  160.5 0.8 copy-start
  165.9 3.6 copy-start.6
  174.2 2.2 copy-start.5
  180.5 0.8 copy-start
  193.3 3.6 copy-start.6
  201.6 2.2 copy-start.5
  206.0 0.8 copy-start
  218.8 3.6 copy-start.6
  227.1 2.2 copy-start.5
  231.5 0.8 copy-start
  236.9 3.6 copy-start.6
  245.2 2.2 copy-start.5
  255.0 3.6 copy-start.6
  263.3 2.2 copy-start.5
  267.7 0.8 copy-start
  273.1 3.6 copy-start.6
  281.4 2.2 copy-start.5
  291.2 3.6 copy-start.6
  299.5 2.2 copy-start.5
  309.3 3.6 copy-start.6
  317.6 2.2 copy-start.5
  327.4 3.6 copy-start.6
  335.8 2.2 copy-start.5
  340.1 0.8 copy-start
  345.6 3.6 copy-start.6
  353.9 2.2 copy-start.5
  358.2 0.8 copy-start
  363.7 3.6 copy-start.6
  372.0 2.2 copy-start.5
  381.8 3.6 copy-start.6
  390.1 2.2 copy-start.5
  394.5 0.8 copy-start
  399.9 3.6 copy-start.6
  408.2 2.2 copy-start.5
  418.0 3.6 copy-start.6
  426.3 2.2 copy-start.5
  430.7 0.8 copy-start
  436.1 3.6 copy-start.6
  455.0 1.2 copy-start.3
  455.0 229.3 %reduce-scatter.5.cloned.1.call-start = ((), (), s32[]{:S(2)}) async-start(), calls=%async_computation.6 | async-start | bytes 5242880 | tf_op jit(solution)/shard_map/reduce_scatter | solution.py:139
  459.5 6.0 collective-permute-start
  471.0 1.2 copy-start.2
  471.0 1.3 copy-start.7
  (6 other events, 4.8 us)
Sparse Core Ops, SparseCore 0:
  10.4 46.3 all-gather.7
  58.6 40.6 all-gather.3
  101.1 40.6 all-gather.5
  455.1 175.7 reduce-scatter.2
  633.3 50.9 reduce-scatter.4
where the time goes:
time: 695 us; the launch traced here: 693 us
  waiting for transfers between devices  336 us (48%)
  other arithmetic  153 us (22%)
  matrix products  127 us (18%)
  local copies, waits for them, and re-layouts  56.4 us (8%)
  between operations  13.8 us (2%)
    reduce_scatter x1, waiting for transfers between devices, on_device(): lax.psum_scatter(lag_parts.reshape(1, panel_count * panel_len, chan_width...  155 us
    dot_general x32, matrix products, spectrum(): jnp.dot(forward_table, panel_rows.astype(jnp.float32), precision=HIGHER)  95.2 us
    add x15, other arithmetic, lag_step(): forward_sum + spec_product(filter_full, signal_spec, interior, False)  54.5 us
    reduce_scatter x1, waiting for transfers between devices, on_device(): lax.psum_scatter(partial_sums[None], 'chan', scatter_dimension=2, tiled=T...  51.6 us
    sub x15, other arithmetic, spec_product(): real_part = left_real * right_real - interior * left_imag * right_imag  47.5 us
    all_gather x1, waiting for transfers between devices, on_device(): lax.all_gather(signal, 'seq', axis=1, tiled=True)  42.5 us
    all_gather x1, waiting for transfers between devices, on_device(): lax.all_gather(long_filter, 'seq', axis=1, tiled=True)  42.5 us
    all_gather x1, waiting for transfers between devices, on_device(): lax.all_gather(gated[None], 'seq', axis=1, tiled=True)  40.3 us
  transfers between devices with their start and end apart: 6, of which 6 were waited for; matrix products, arithmetic and copies ran while one was open for 3% of the time, Pallas kernels for 0%

commit v1 on v0

--- a/solution.py
+++ b/solution.py
@@ -6,6 +6,27 @@
 
 HIGHEST = lax.Precision.HIGHEST
 HIGHER = lax.Precision.HIGH
+
+
+def ring_gather(value, axis, dim):
+    devices, index, rows = (lax.axis_size(axis), lax.axis_index(axis), value.shape[dim])
+    right = [(i, (i + 1) % devices) for i in range(devices)]
+    left = [(i, (i - 1) % devices) for i in range(devices)]
+    filled = jnp.zeros((*value.shape[:dim], devices * rows, *value.shape[dim + 1 :]), value.dtype)
+    filled = lax.dynamic_update_slice_in_dim(filled, value, index * rows, axis=dim)
+    from_left = from_right = value
+    half = devices // 2
+    for step in range(1, half + 1):
+        from_left = lax.ppermute(from_left, axis, right)
+        filled = lax.dynamic_update_slice_in_dim(
+            filled, from_left, (index - step) % devices * rows, axis=dim
+        )
+        if step < devices - half:
+            from_right = lax.ppermute(from_right, axis, left)
+            filled = lax.dynamic_update_slice_in_dim(
+                filled, from_right, (index + step) % devices * rows, axis=dim
+            )
+    return filled
 
 
 def passed_along(x, axis, by):
@@ -61,7 +82,7 @@
     signals, gateds, filters = (
         lax.all_gather(signal, "seq", axis=1, tiled=True),
         lax.all_gather(gated[None], "seq", axis=1, tiled=True),
-        lax.all_gather(long_filter, "seq", axis=1, tiled=True),
+        ring_gather(long_filter, "seq", 1),
     )
     zero_spec = jnp.zeros((span_len, chan_width), jnp.float32)
 

time: 695 us -> 655 us (0.942)
  waiting for transfers between devices: 336 us -> 252 us
  starting transfers between devices: 2.92 us -> 34 us
  local copies, waits for them, and re-layouts: 56.4 us -> 69.1 us
    all_gather x1 -> x0, waiting for transfers between devices: 42.5 us -> none  [on_device(): lax.all_gather(long_filter, 'seq', axis=1, tiled=True)]
    all_gather x1, waiting for transfers between devices: 40.3 us -> 0.01 us  [on_device(): lax.all_gather(gated[None], 'seq', axis=1, tiled=True)]
    ppermute x0 -> x15, starting transfers between devices: none -> 31.4 us  [the longest x7 25.1 us: ring_gather(): from_right = lax.ppermute(from_right, axis, left)]
    ppermute x0 -> x15, waiting for transfers between devices: none -> 14.9 us  [the longest x7 7.61 us: ring_gather(): from_right = lax.ppermute(from_right, axis, left)]
    all_gather x1, waiting for transfers between devices: 42.5 us -> 27.7 us  [on_device(): lax.all_gather(signal, 'seq', axis=1, tiled=True)]
    dynamic_update_slice x0 -> x16, local copies, waits for them, and re-layouts: none -> 11.6 us  [the longest x8 5.76 us: ring_gather(): lax.dynamic_update_slice_in_dim(filled, from_left, (index - step) % devic...]
  transfers between devices with their start and end apart: 6 -> 20, of which waited for: 6 -> 10; matrix products, arithmetic and copies ran while one was open for 3% -> 5% of each run, Pallas kernels for 0% -> 0%
where the time goes in v1:
time: 655 us; the launch traced here: 652 us
  waiting for transfers between devices  252 us (38%)
  other arithmetic  153 us (23%)
  matrix products  127 us (19%)
  local copies, waits for them, and re-layouts  69.1 us (11%)
  starting transfers between devices  34 us (5%)
  between operations  13.9 us (2%)
    reduce_scatter x1, waiting for transfers between devices, on_device(): lax.psum_scatter(lag_parts.reshape(1, panel_count * panel_len, chan_width...  154 us
    dot_general x32, matrix products, spectrum(): jnp.dot(forward_table, panel_rows.astype(jnp.float32), precision=HIGHER)  94.8 us
    add x15, other arithmetic, lag_step(): forward_sum + spec_product(filter_full, signal_spec, interior, False)  54.6 us
    reduce_scatter x1, waiting for transfers between devices, on_device(): lax.psum_scatter(partial_sums[None], 'chan', scatter_dimension=2, tiled=T...  51.7 us
    sub x15, other arithmetic, spec_product(): real_part = left_real * right_real - interior * left_imag * right_imag  47.5 us
    select_n x15, other arithmetic, make_tables(): jnp.where(row_index <= panel_len, jnp.cos(angles), -jnp.sin(angles))  33 us
    all_gather x1, waiting for transfers between devices, on_device(): lax.all_gather(signal, 'seq', axis=1, tiled=True)  27.7 us
    while x105, local copies, waits for them, and re-layouts  26 us
  transfers between devices with their start and end apart: 20, of which 10 were waited for; matrix products, arithmetic and copies ran while one was open for 5% of the time, Pallas kernels for 0%

profile of v1, /device:TPU:1, one launch (start us, length us, event | category | flops | bytes accessed | tf_op | source)
XLA Modules:
  0.0 652.5 jit_solution(1543392495552423793)
XLA Ops:
  20.9 4.8 fusion.62
  26.8 3.8 collective-permute-start.5
  37.1 4.4 collective-permute-start.7
  47.0 6.4 collective-permute-start.9
  57.6 3.8 collective-permute-start.11
  63.5 4.8 collective-permute-start.13
  71.2 3.9 collective-permute-done.14
  75.9 27.7 %all-gather.3.cloned.1.call-done = bf16[1,4096,512]{2,1,0:T(8,128)(2,1)} async-done(((bf16[1,256,512]{2,1,0:T(8,128)(2,1)}), bf16[1,4096,512]{2,1,0:T(8,128)(2,1)}) %all-gather.3.cloned.1.call-update) | async-done | bytes 4194320 | tf_op jit(solution)/shard_map/all_gather | solution.py:83
  103.6 4.2 broadcast_in_dim.41
  111.2 289.0 %while.31 = (s32[]{:T(128)}, f32[512,512]{1,0:T(8,128)S(1)}, f32[512,512]{1,0:T(8,128)}, f32[512,512]{1,0:T(8,128)}, f32[512,512]{1,0:T(8,128)}, /*index=5*/pred...) while((s32[]{:T(128)}, f32[512,512]{1,0:T(8,128)S(1)}, ...), condition=%wide.region_7.8_spmd.clone.clone.clone, body=%wide.region_0.7_spmd.clone.clone.clone.sunk | while | flops 2027169536 | bytes 49307344 | solution.py:142
  111.2 4.6 multiply_add_fusion.5
  127.5 3.6 maximum_add_fusion.3
  131.1 4.6 multiply_add_fusion.5
  146.4 7.4 %conditional.19 = (f32[16,256,512]{1,2,0:T(8,128)}) conditional(s32[]{:T(128)} %convert_element_type.270, f32[16,256,512]{1,2,0:T(8,128)} %get-tuple-element.824, (s32[]{:T(128)}, f32[16,256,512]{1,2,0:T(8,128)}, f32[512,1]{0,1:T(1,128)S(1)}, f32[512,512]{1,0:T(8,128)S(1)}, f32[512,512]{1,0:T(8,128)}, /*index=5*/pred[256,512]{1,0:T(32,128)(4,1)S(1)}, ...), branch_computations={%region_5.5_spmd, %region_6.6_spmd} | conditional | flops 806354944 | bytes 4329508 | solution.py:113
  146.4 7.4 %fusion.15 = f32[16,256,512]{1,2,0:T(8,128)} fusion(f32[16,256,512]{1,2,0:T(8,128)} %get-tuple-element.344, s32[]{:T(128)S(6)} %max.13, f32[512,512]{1,0:T(8,128)} %get-tuple-element.346, f32[512,512]{1,0:T(8,128)S(1)} %get-tuple-element.348, pred[256,512]{1,0:T(32,128)(4,1)S(1)} %get-tuple-element.581, f32[256,512]{1,0:T(8,128)S(1)} %get-tuple-element.587, ...), kind=kOutput, calls=%fused_computation.14 | convolution fusion | flops 806354944 | bytes 4329476 | tf_op jit(solution)/shard_map/while/body/cond/branch_1_fun/dot_general | solution.py:102
  154.8 3.6 maximum_add_fusion.3
  158.4 4.6 multiply_add_fusion.5
  171.8 7.4 %conditional.19 = (f32[16,256,512]{1,2,0:T(8,128)}) conditional(s32[]{:T(128)} %convert_element_type.270, f32[16,256,512]{1,2,0:T(8,128)} %get-tuple-element.824, (s32[]{:T(128)}, f32[16,256,512]{1,2,0:T(8,128)}, f32[512,1]{0,1:T(1,128)S(1)}, f32[512,512]{1,0:T(8,128)S(1)}, f32[512,512]{1,0:T(8,128)}, /*index=5*/pred[256,512]{1,0:T(32,128)(4,1)S(1)}, ...), branch_computations={%region_5.5_spmd, %region_6.6_spmd} | conditional | flops 806354944 | bytes 4329508 | solution.py:113
  171.8 7.4 %fusion.15 = f32[16,256,512]{1,2,0:T(8,128)} fusion(f32[16,256,512]{1,2,0:T(8,128)} %get-tuple-element.344, s32[]{:T(128)S(6)} %max.13, f32[512,512]{1,0:T(8,128)} %get-tuple-element.346, f32[512,512]{1,0:T(8,128)S(1)} %get-tuple-element.348, pred[256,512]{1,0:T(32,128)(4,1)S(1)} %get-tuple-element.581, f32[256,512]{1,0:T(8,128)S(1)} %get-tuple-element.587, ...), kind=kOutput, calls=%fused_computation.14 | convolution fusion | flops 806354944 | bytes 4329476 | tf_op jit(solution)/shard_map/while/body/cond/branch_1_fun/dot_general | solution.py:102
  180.2 3.6 maximum_add_fusion.3
  183.9 4.6 multiply_add_fusion.5
  198.2 3.6 maximum_add_fusion.3
  201.9 4.6 multiply_add_fusion.5
  216.2 3.6 maximum_add_fusion.3
  219.9 4.6 multiply_add_fusion.5
  234.3 3.6 maximum_add_fusion.3
  237.9 4.6 multiply_add_fusion.5
  252.3 3.6 maximum_add_fusion.3
  256.0 4.6 multiply_add_fusion.5
  270.3 3.6 maximum_add_fusion.3
  274.0 4.6 multiply_add_fusion.5
  288.4 3.6 maximum_add_fusion.3
  292.0 4.6 multiply_add_fusion.5
  306.4 3.6 maximum_add_fusion.3
  310.0 4.6 multiply_add_fusion.5
  324.4 3.6 maximum_add_fusion.3
  328.1 4.6 multiply_add_fusion.5
  346.1 4.6 multiply_add_fusion.5
  364.1 4.6 multiply_add_fusion.5
  382.2 4.6 multiply_add_fusion.5
  396.5 3.6 maximum_add_fusion.3
  400.2 9.3 %conditional.4 = (f32[16,256,512]{2,1,0:T(8,128)}) conditional(s32[]{:T(128)} %convert_element_type.151, (f32[16,256,512]{1,2,0:T(8,128)}) %tuple.109, (s32[]{:T(128)}, f32[16,256,512]{1,2,0:T(8,128)}, pred[256,512]{1,0:T(32,128)(4,1)S(1)}, f32[512,512]{1,0:T(8,128)}, f32[512]{0:T(512)S(1)}, /*index=5*/f32[256,512]{1,0:T(8,128)}, ...), branch_computations={%region_8.9_spmd, %region_9.10_spmd} | conditional | flops 805830656 | bytes 26347600 | solution.py:113
  400.2 9.2 %copy.46 = f32[16,256,512]{2,1,0:T(8,128)} copy(f32[16,256,512]{1,2,0:T(8,128)} %get-tuple-element.589) | data formatting | bytes 16777216 | tf_op jit(solution)/shard_map/while | solution.py:142
  409.5 5.9 convert_element_type.152
  425.6 5.5 convolution_bitcast_fusion.5
  432.4 4.0 fusion.50
  436.4 154.0 %reduce-scatter.3.cloned.1.call-done = bf16[1,256,512]{2,1,0:T(8,128)(2,1)} async-done(((bf16[1,4096,512]{2,1,0:T(8,128)(2,1)}), bf16[1,256,512]{2,1,0:T(8,128)(2,1)}) %reduce-scatter.3.cloned.1.call-update) | async-done | bytes 262160 | tf_op jit(solution)/shard_map/reduce_scatter | solution.py:147
  592.2 51.7 %reduce-scatter.5.cloned.1.call-done = f32[1,256,1024]{2,1,0:T(8,128)} async-done(((f32[1,256,4096]{2,1,0:T(8,128)}), f32[1,256,1024]{2,1,0:T(8,128)}) %reduce-scatter.5.cloned.1.call-update) | async-done | bytes 1048592 | tf_op jit(solution)/shard_map/reduce_scatter | solution.py:160
  (438 shorter events, 249.3 us)
Async XLA Ops:
  7.2 68.7 %all-gather.5.cloned.1.call-start = ((), (), s32[]{:S(2)}) async-start(), calls=%async_computation.3 | async-start | bytes 4456448 | tf_op jit(solution)/shard_map/all_gather | solution.py:84
  9.0 23.8 %copy-start.8 = (bf16[1,256,512]{2,1,0:T(8,128)(2,1)S(1)}, bf16[1,256,512]{2,1,0:T(8,128)(2,1)}, u32[]{:S(2)}) copy-start(bf16[1,256,512]{2,1,0:T(8,128)(2,1)} %param.18) | copy-start | bytes 786436
  9.0 94.5 %all-gather.3.cloned.1.call-start = ((), (), s32[]{:S(2)}) async-start(), calls=%async_computation.2 | async-start | bytes 4456448 | tf_op jit(solution)/shard_map/all_gather | solution.py:83
  9.8 580.6 %reduce-scatter.3.cloned.1.call-start = ((), (), s32[]{:S(2)}) async-start(), calls=%async_computation.4 | async-start | bytes 4456448 | tf_op jit(solution)/shard_map/reduce_scatter | solution.py:147
  9.8 6.7 %collective-permute-start = (bf16[1,256,512]{2,1,0:T(8,128)(2,1)}, bf16[1,256,512]{2,1,0:T(8,128)(2,1)S(1)}, u32[]{:S(2)}, u32[]{:S(2)}) collective-permute-start(bf16[1,256,512]{2,1,0:T(8,128)(2,1)} %param.18), channel_id=1, source_target_pairs={{0,4},{4,8},{8,12},{12,16},{16,20},{20,24},{24,28},{28,32},{32,36}... | collective-permute-start | bytes 786440 | tf_op jit(solution)/shard_map/ppermute | solution.py:20
  12.9 6.3 collective-permute-start.1
  16.5 9.2 %collective-permute-start.2 = (bf16[1,256,512]{2,1,0:T(8,128)(2,1)S(1)}, bf16[1,256,512]{2,1,0:T(8,128)(2,1)S(1)}, u32[]{:S(2)}, u32[]{:S(2)}) collective-permute-start(bf16[1,256,512]{2,1,0:T(8,128)(2,1)S(1)} %collective-permute-done), channel_id=1, source_target_pairs={{0,4},{4,8},{8,12},{12,16},{16,20},{20,24},{24,28},{28,32},{32,36}... | collective-permute-start | bytes 786440 | tf_op jit(solution)/shard_map/ppermute | solution.py:20
  19.2 7.6 %collective-permute-start.3 = (bf16[1,256,512]{2,1,0:T(8,128)(2,1)S(1)}, bf16[1,256,512]{2,1,0:T(8,128)(2,1)S(1)}, u32[]{:S(2)}, u32[]{:S(2)}) collective-permute-start(bf16[1,256,512]{2,1,0:T(8,128)(2,1)S(1)} %collective-permute-done.1), channel_id=1, source_target_pairs={{0,60},{4,0},{8,4},{12,8},{16,12},{20,16},{24,20},{28,24},{32,28},... | collective-permute-start | bytes 786440 | tf_op jit(solution)/shard_map/ppermute | solution.py:25
  25.7 7.9 %collective-permute-start.4 = (bf16[1,256,512]{2,1,0:T(8,128)(2,1)S(1)}, bf16[1,256,512]{2,1,0:T(8,128)(2,1)S(1)}, u32[]{:S(2)}, u32[]{:S(2)}) collective-permute-start(bf16[1,256,512]{2,1,0:T(8,128)(2,1)S(1)} %collective-permute-done.2), channel_id=1, source_target_pairs={{0,4},{4,8},{8,12},{12,16},{16,20},{20,24},{24,28},{28,32},{32,36}... | collective-permute-start | bytes 786440 | tf_op jit(solution)/shard_map/ppermute | solution.py:20
  26.8 10.4 %collective-permute-start.5 = (bf16[1,256,512]{2,1,0:T(8,128)(2,1)S(1)}, bf16[1,256,512]{2,1,0:T(8,128)(2,1)S(1)}, u32[]{:S(2)}, u32[]{:S(2)}) collective-permute-start(bf16[1,256,512]{2,1,0:T(8,128)(2,1)S(1)} %collective-permute-done.3), channel_id=1, source_target_pairs={{0,60},{4,0},{8,4},{12,8},{16,12},{20,16},{24,20},{28,24},{32,28},... | collective-permute-start | bytes 786440 | tf_op jit(solution)/shard_map/ppermute | solution.py:25
  33.6 8.7 %collective-permute-start.6 = (bf16[1,256,512]{2,1,0:T(8,128)(2,1)S(1)}, bf16[1,256,512]{2,1,0:T(8,128)(2,1)S(1)}, u32[]{:S(2)}, u32[]{:S(2)}) collective-permute-start(bf16[1,256,512]{2,1,0:T(8,128)(2,1)S(1)} %collective-permute-done.4), channel_id=1, source_target_pairs={{0,4},{4,8},{8,12},{12,16},{16,20},{20,24},{24,28},{28,32},{32,36}... | collective-permute-start | bytes 786440 | tf_op jit(solution)/shard_map/ppermute | solution.py:20
  37.1 9.8 %collective-permute-start.7 = (bf16[1,256,512]{2,1,0:T(8,128)(2,1)S(1)}, bf16[1,256,512]{2,1,0:T(8,128)(2,1)S(1)}, u32[]{:S(2)}, u32[]{:S(2)}) collective-permute-start(bf16[1,256,512]{2,1,0:T(8,128)(2,1)S(1)} %collective-permute-done.5), channel_id=1, source_target_pairs={{0,60},{4,0},{8,4},{12,8},{16,12},{20,16},{24,20},{28,24},{32,28},... | collective-permute-start | bytes 786440 | tf_op jit(solution)/shard_map/ppermute | solution.py:25
  42.2 11.8 %collective-permute-start.8 = (bf16[1,256,512]{2,1,0:T(8,128)(2,1)S(1)}, bf16[1,256,512]{2,1,0:T(8,128)(2,1)S(1)}, u32[]{:S(2)}, u32[]{:S(2)}) collective-permute-start(bf16[1,256,512]{2,1,0:T(8,128)(2,1)S(1)} %collective-permute-done.6), channel_id=1, source_target_pairs={{0,4},{4,8},{8,12},{12,16},{16,20},{20,24},{24,28},{28,32},{32,36}... | collective-permute-start | bytes 786440 | tf_op jit(solution)/shard_map/ppermute | solution.py:20
  47.0 10.6 %collective-permute-start.9 = (bf16[1,256,512]{2,1,0:T(8,128)(2,1)S(1)}, bf16[1,256,512]{2,1,0:T(8,128)(2,1)S(1)}, u32[]{:S(2)}, u32[]{:S(2)}) collective-permute-start(bf16[1,256,512]{2,1,0:T(8,128)(2,1)S(1)} %collective-permute-done.7), channel_id=1, source_target_pairs={{0,60},{4,0},{8,4},{12,8},{16,12},{20,16},{24,20},{28,24},{32,28},... | collective-permute-start | bytes 786440 | tf_op jit(solution)/shard_map/ppermute | solution.py:25
  54.1 8.0 %collective-permute-start.10 = (bf16[1,256,512]{2,1,0:T(8,128)(2,1)S(1)}, bf16[1,256,512]{2,1,0:T(8,128)(2,1)S(1)}, u32[]{:S(2)}, u32[]{:S(2)}) collective-permute-start(bf16[1,256,512]{2,1,0:T(8,128)(2,1)S(1)} %collective-permute-done.8), channel_id=1, source_target_pairs={{0,4},{4,8},{8,12},{12,16},{16,20},{20,24},{24,28},{28,32},{32,36}... | collective-permute-start | bytes 786440 | tf_op jit(solution)/shard_map/ppermute | solution.py:20
  57.6 6.0 collective-permute-start.11
  62.1 7.0 %collective-permute-start.12 = (bf16[1,256,512]{2,1,0:T(8,128)(2,1)S(1)}, bf16[1,256,512]{2,1,0:T(8,128)(2,1)S(1)}, u32[]{:S(2)}, u32[]{:S(2)}) collective-permute-start(bf16[1,256,512]{2,1,0:T(8,128)(2,1)S(1)} %collective-permute-done.10), channel_id=1, source_target_pairs={{0,4},{4,8},{8,12},{12,16},{16,20},{20,24},{24,28},{28,32},{32,36}... | collective-permute-start | bytes 786440 | tf_op jit(solution)/shard_map/ppermute | solution.py:20
  63.5 7.0 %collective-permute-start.13 = (bf16[1,256,512]{2,1,0:T(8,128)(2,1)S(1)}, bf16[1,256,512]{2,1,0:T(8,128)(2,1)S(1)}, u32[]{:S(2)}, u32[]{:S(2)}) collective-permute-start(bf16[1,256,512]{2,1,0:T(8,128)(2,1)S(1)} %collective-permute-done.11), channel_id=1, source_target_pairs={{0,60},{4,0},{8,4},{12,8},{16,12},{20,16},{24,20},{28,24},{32,28},... | collective-permute-start | bytes 786440 | tf_op jit(solution)/shard_map/ppermute | solution.py:25
  69.1 6.1 collective-permute-start.14
  115.9 2.2 copy-start.5
  127.5 3.6 copy-start.6
  154.8 3.6 copy-start.6
  163.1 2.2 copy-start.5
  180.2 3.6 copy-start.6
  188.5 2.2 copy-start.5
  198.2 3.6 copy-start.6
  206.5 2.2 copy-start.5
  216.2 3.6 copy-start.6
  224.5 2.2 copy-start.5
  234.3 3.6 copy-start.6
  242.6 2.2 copy-start.5
  252.3 3.6 copy-start.6
  260.6 2.2 copy-start.5
  270.3 3.6 copy-start.6
  278.6 2.2 copy-start.5
  288.4 3.6 copy-start.6
  296.7 2.2 copy-start.5
  306.4 3.6 copy-start.6
  314.7 2.2 copy-start.5
  324.4 3.6 copy-start.6
  332.7 2.2 copy-start.5
  342.4 3.6 copy-start.6
  350.7 2.2 copy-start.5
  360.5 3.6 copy-start.6
  378.5 3.6 copy-start.6
  396.5 3.6 copy-start.6
  415.4 228.4 %reduce-scatter.5.cloned.1.call-start = ((), (), s32[]{:S(2)}) async-start(), calls=%async_computation.5 | async-start | bytes 5242880 | tf_op jit(solution)/shard_map/reduce_scatter | solution.py:160
  419.9 5.7 collective-permute-start.15
  (21 other events, 22.3 us)
Sparse Core Ops, SparseCore 0:
  10.4 49.8 all-gather.4
  62.1 41.4 all-gather.2
  415.5 174.7 reduce-scatter.2
  592.8 51.0 reduce-scatter.4
